TPU v7x, 256 devices: a whole 4x4x8 slice. The times are simulated.
256 devices in a mesh: rows: 32 (over z, y), samp: 8 (over x, core).
Axes of the slice: x: 4, y: 4, z: 8, core: 2. Of those that a mesh axis runs over, the one named last changes fastest.
Arguments:
- coupling_tiles: bfloat16 [512, 32, 128, 128], P('rows', 'samp'), may hold values from -0.09375 to 0.09375
- tile_columns: int32 [512, 32], P('rows', 'samp'), may hold values from 0 to 511, as said below
- sample_matrix: bfloat16 [65536, 512], P('rows'), may hold values from -6 to 6
- phi_leaf: float32 [512, 256], replicated, may hold values from -0.25 to 0.25
- phi_pair: float32 [512, 256], replicated, may hold values from -0.25 to 0.25
- phi_quad: float32 [512, 256], replicated, may hold values from -0.25 to 0.25
Outputs:
- leaf_basis: float32 [65536, 256], P('rows')
- nested_transfer: float32 [8192, 256], P('rows')
- sample_approx: float32 [65536, 512], P('rows', 'samp')
Inputs may be any that keep to these rules, and one draw needn't show every extreme that they name: `tile_columns`: the 32 tile columns of a tile row are distinct and lie in the leaf block of that row or in one of the two leaf blocks beside it (16 tile rows to a leaf block).
All inputs are finite; a program needn't handle non-finite values.
Results may differ from a plain program's by a relative error of at most 0.0003.
Values may be sent and summed in bfloat16 or wider, within the bound.
A program may use at most 128 MiB of HBM per device.

v0:
```python
import jax
import jax.numpy as jnp
from jax import lax
from jax.sharding import PartitionSpec as P

NS_ITERS = 5
HIGH = lax.Precision.HIGHEST


def with_halo(block, sides, width):
    for axis, dim in sides:
        count = lax.axis_size(axis)
        forward = [(i, i + 1) for i in range(count - 1)]
        backward = [(target, source) for source, target in forward]
        low = lax.ppermute(
            lax.slice_in_dim(block, block.shape[dim] - width, None, axis=dim), axis, forward
        )
        high = lax.ppermute(lax.slice_in_dim(block, 0, width, axis=dim), axis, backward)
        block = jnp.concatenate([low, block, high], axis=dim)
    return block


def swapped(value, axis, distance):
    return lax.ppermute(value, axis, [(i, i ^ 1 << distance) for i in range(lax.axis_size(axis))])


def product(left, right):
    return jnp.dot(left, right, precision=HIGH, preferred_element_type=jnp.float32)


def orthogonal(matrix):
    gram_matrix = product(matrix.T, matrix)
    norm_scale = jnp.sqrt(jnp.sum(gram_matrix * gram_matrix)) + 1e-06
    identity = jnp.eye(gram_matrix.shape[0], dtype=jnp.float32)
    iterate = gram_matrix / norm_scale
    inverse_root = identity
    for step in range(NS_ITERS):
        factor = 1.5 * identity - 0.5 * product(inverse_root, iterate)
        iterate = product(iterate, factor)
        inverse_root = product(factor, inverse_root)
    return product(matrix, inverse_root) / jnp.sqrt(norm_scale)


def stack_pair(mine, other, which_bit):
    lower = jnp.where(which_bit == 0, mine, other)
    higher = jnp.where(which_bit == 0, other, mine)
    return jnp.concatenate([lower, higher], axis=0)


def on_device(coupling_tiles, tile_columns, sample_matrix, phi_leaf, phi_pair, phi_quad):
    per_leaf = 16
    leaf_rows = sample_matrix.shape[0]
    sample_cols = sample_matrix.shape[1]
    row_index = lax.axis_index("rows")
    extended = with_halo(sample_matrix, (("rows", 0),), leaf_rows)
    blocks = extended.reshape(3 * per_leaf, leaf_rows // per_leaf, sample_cols)
    local_columns = tile_columns - (row_index - 1) * per_leaf
    picked = jnp.take(blocks, local_columns, axis=0)
    partial_value = jnp.einsum(
        "tkab,tkbs->tas", coupling_tiles, picked, preferred_element_type=jnp.float32
    )
    partial_value = partial_value.reshape(leaf_rows, sample_cols)
    samp_count = lax.axis_size("samp")
    samp_index = lax.axis_index("samp")
    share_cols = sample_cols // samp_count
    sample = lax.psum(partial_value, "samp")

    def sketch(stacked, phi_matrix):
        return product(stacked, phi_matrix)

    def merge_level(stacked, phi_matrix):
        basis_now = orthogonal(sketch(stacked, phi_matrix))
        return (basis_now, product(basis_now.T, stacked))

    basis, coarse = merge_level(sample, phi_leaf)
    sibling_bit = row_index % 2
    cousin_bit = row_index // 2 % 2
    pair = stack_pair(coarse, swapped(coarse, "rows", 0), sibling_bit)
    upper, middle = merge_level(pair, phi_pair)
    quad = stack_pair(middle, swapped(middle, "rows", 1), cousin_bit)
    top, summary = merge_level(quad, phi_quad)
    rank_leaf = coarse.shape[0]
    rank_pair = middle.shape[0]
    own_upper = lax.dynamic_slice_in_dim(upper, sibling_bit * rank_leaf, rank_leaf, 0)
    own_top = lax.dynamic_slice_in_dim(top, cousin_bit * rank_pair, rank_pair, 0)
    nested = product(own_upper, own_top)
    approx = product(
        basis,
        product(nested, lax.dynamic_slice_in_dim(summary, samp_index * share_cols, share_cols, 1)),
    )
    return (basis, nested, approx)


def solution(mesh):
    return jax.shard_map(
        on_device,
        mesh=mesh,
        in_specs=(P("rows", "samp", None, None), P("rows", "samp"), P("rows", None), P(), P(), P()),
        out_specs=(P("rows", None), P("rows", None), P("rows", "samp")),
        check_vma=False,
    )
```

profile of v0, /device:TPU:7, one launch (start us, length us, event | category | flops | bytes accessed | tf_op | source)
XLA Modules:
  0.0 261.3 jit_solution(8823519993755245035)
XLA Ops:
  7.2 4.7 %collective-permute-start = (bf16[2048,512]{1,0:T(8,128)(2,1)}, bf16[2048,512]{1,0:T(8,128)(2,1)}, u32[]{:S(2)}, u32[]{:S(2)}) collective-permute-start(bf16[2048,512]{1,0:T(8,128)(2,1)} %param.8), channel_id=1, source_target_pairs={{0,8},{8,16},{16,24},{24,32},{32,40},{40,48},{48,56},{56,64},{64,7... | collective-permute-start | bytes 6291464 | tf_op jit(solution)/shard_map/ppermute | solution.py:15
  11.9 1.3 collective-permute-start.1
  13.2 0.7 compare_and_fusion
  14.1 41.0 %collective-permute-done = bf16[2048,512]{1,0:T(8,128)(2,1)} collective-permute-done((bf16[2048,512]{1,0:T(8,128)(2,1)}, bf16[2048,512]{1,0:T(8,128)(2,1)}, u32[]{:S(2)}, u32[]{:S(2)}) %collective-permute-start) | collective-permute-done | bytes 2097184 | tf_op jit(solution)/shard_map/ppermute | solution.py:15
  55.2 5.1 %collective-permute-done.1 = bf16[2048,512]{1,0:T(8,128)(2,1)} collective-permute-done((bf16[2048,512]{1,0:T(8,128)(2,1)}, bf16[2048,512]{1,0:T(8,128)(2,1)}, u32[]{:S(2)}, u32[]{:S(2)}) %collective-permute-start.1) | collective-permute-done | bytes 2097184 | tf_op jit(solution)/shard_map/ppermute | solution.py:18
  60.3 6.0 %pad_maximum_fusion = bf16[6144,512]{1,0:T(8,128)(2,1)} fusion(bf16[2048,512]{1,0:T(8,128)(2,1)} %collective-permute-done.1, bf16[2048,512]{1,0:T(8,128)(2,1)} %param.8, bf16[2048,512]{1,0:T(8,128)(2,1)} %collective-permute-done), kind=kLoop, calls=%fused_computation.4 | loop fusion | flops 18874368 | bytes 12582912 | tf_op jit(solution)/shard_map/concatenate | solution.py:19
  66.2 8.3 %gather_fusion = bf16[64,128,512]{2,1,0:T(8,128)(2,1)} fusion(bf16[48,128,512]{2,1,0:T(8,128)(2,1)} %bitcast.104, s32[1024]{0:T(1024)S(1)} %pad_clamp_fusion), kind=kCustom, calls=%fused_computation | custom fusion | bytes 16777472 | tf_op jit(solution)/shard_map/jit(_take)/gather | solution.py:58
  74.6 7.1 %fusion = f32[16,512,128,1]{1,2,3,0:T(8,128)} fusion(bf16[16,4,128,128]{3,2,1,0:T(8,128)(2,1)S(1)} %copy-done, bf16[16,4,128,512]{3,2,1,0:T(8,128)(2,1)} %bitcast.105, pred[16,4]{1,0:T(8,128)(4,1)S(1)} %copy.11), kind=kOutput, calls=%fused_computation.1 | convolution fusion | flops 1077936128 | bytes 14680128 | tf_op jit(solution)/shard_map/tkab,tkbs->tas/dot_general | solution.py:59
  81.7 81.9 %all-reduce.2.cloned.1.call-done = f32[2048,512]{1,0:T(8,128)} async-done(((f32[2048,512]{1,0:T(8,128)}), f32[2048,512]{1,0:T(8,128)}) %all-reduce.2.cloned.1.call-update) | async-done | bytes 4194320 | tf_op jit(solution)/shard_map/psum | solution.py:66
  163.6 5.7 %fusion.26 = f32[2048,256]{1,0:T(8,128)S(1)} fusion(f32[2048,512]{1,0:T(8,128)} %all-reduce.2.cloned.1.call-done, f32[512,256]{1,0:T(8,128)S(1)} %copy-done.11), kind=kOutput, calls=%fused_computation.77 | convolution fusion | flops 3221225472 | bytes 6815744 | tf_op jit(solution)/shard_map/dot_general | solution.py:28
  169.3 1.3 copy-done.1
  170.7 4.2 %multiply_reduce_fusion.2 = (f32[]{:T(128)}, f32[256,256]{1,0:T(8,128)S(1)}) fusion(f32[2048,256]{1,0:T(8,128)S(1)} %fusion.26), kind=kOutput, calls=%fused_computation.50 | convolution fusion | flops 1610743808 | bytes 2359300 | tf_op jit(solution)/shard_map/dot_general | solution.py:28
  175.9 0.4 fusion.16
  176.5 0.4 select_subtract_fusion.13
  178.9 0.4 select_subtract_fusion.11
  180.1 0.4 select_subtract_fusion.10
  180.9 3.7 %convolution_divide_fusion = f32[2048,256]{1,0:T(8,128)S(1)} fusion(f32[2048,256]{1,0:T(8,128)} %copy-done.1, f32[256,256]{1,0:T(8,128)S(1)} %fusion.33, f32[]{:T(128)S(6)} %sqrt.19), kind=kOutput, calls=%fused_computation.6 | convolution fusion | flops 1611137024 | bytes 4456452 | tf_op jit(solution)/shard_map/dot_general | solution.py:28
  184.6 4.0 %fusion.34 = f32[256,512]{1,0:T(8,128)S(1)} fusion(f32[2048,256]{1,0:T(8,128)S(1)} %convolution_divide_fusion, f32[2048,512]{1,0:T(8,128)S(1)} %copy-done.2), kind=kOutput, calls=%fused_computation.85 | convolution fusion | flops 3221225472 | bytes 6815744 | tf_op jit(solution)/shard_map/dot_general | solution.py:28
  188.6 1.3 collective-permute-start.2
  189.9 11.4 %collective-permute-done.2 = f32[256,512]{1,0:T(8,128)} collective-permute-done((f32[256,512]{1,0:T(8,128)S(1)}, f32[256,512]{1,0:T(8,128)}, u32[]{:S(2)}, u32[]{:S(2)}) %collective-permute-start.2) | collective-permute-done | bytes 524320 | tf_op jit(solution)/shard_map/ppermute | solution.py:24
  201.3 1.3 broadcast_select_fusion.3
  202.6 2.0 fusion.7
  204.7 0.8 copy-done.6
  205.4 1.6 multiply_reduce_fusion.1
  208.1 0.4 fusion.17
  208.8 0.4 select_subtract_fusion.8
  209.9 0.4 select_subtract_fusion.7
  211.5 1.1 fusion.40
  213.0 1.3 select_subtract_fusion.5
  214.7 1.6 convolution_divide_fusion.2
  216.4 1.9 fusion.6
  218.2 2.9 %collective-permute-start.3 = (f32[256,512]{1,0:T(8,128)}, f32[256,512]{1,0:T(8,128)}, u32[]{:S(2)}, u32[]{:S(2)}) collective-permute-start(f32[256,512]{1,0:T(8,128)} %fusion.6), channel_id=1, source_target_pairs={{0,16},{8,24},{16,0},{24,8},{32,48},{40,56},{48,32},{56,40},{64,80... | collective-permute-start | bytes 1572872 | tf_op jit(solution)/shard_map/ppermute | solution.py:24
  221.1 12.9 %collective-permute-done.3 = f32[256,512]{1,0:T(8,128)} collective-permute-done((f32[256,512]{1,0:T(8,128)}, f32[256,512]{1,0:T(8,128)}, u32[]{:S(2)}, u32[]{:S(2)}) %collective-permute-start.3) | collective-permute-done | bytes 524320 | tf_op jit(solution)/shard_map/ppermute | solution.py:24
  234.1 1.3 broadcast_select_fusion.1
  235.4 2.0 fusion.5
  237.4 0.8 copy-done.5
  238.2 1.6 multiply_reduce_fusion
  240.8 0.4 fusion.18
  241.5 0.4 select_subtract_fusion.3
  242.7 0.4 select_subtract_fusion.2
  243.8 0.4 select_subtract_fusion.1
  244.2 1.1 fusion.47
  245.8 1.5 select_subtract_fusion
  247.7 1.6 convolution_divide_fusion.1
  249.3 1.1 fusion.4
  250.4 0.4 fusion.8
  250.8 0.5 fusion.14
  251.2 3.0 %fusion.49 = f32[2048,64]{0,1:T(8,128)} fusion(f32[2048,256]{1,0:T(8,128)S(1)} %copy-done.4, f32[256,64]{1,0:T(8,128)S(1)} %fusion.14), kind=kOutput, calls=%fused_computation.100 | convolution fusion | flops 402653184 | bytes 2686976 | tf_op jit(solution)/shard_map/dot_general | solution.py:28
  (54 shorter events, 10.1 us)
Async XLA Ops:
  7.2 67.4 %copy-start = (bf16[16,4,128,128]{3,2,1,0:T(8,128)(2,1)S(1)}, bf16[16,4,128,128]{3,2,1,0:T(8,128)(2,1)}, u32[]{:S(2)}) copy-start(bf16[16,4,128,128]{3,2,1,0:T(8,128)(2,1)} %param.6) | copy-start | bytes 6291460
  7.2 156.4 %all-reduce.2.cloned.1.call-start = ((), (), s32[]{:S(2)}) async-start(), calls=%async_computation | async-start | bytes 8388608 | tf_op jit(solution)/shard_map/psum | solution.py:66
  7.2 47.9 %collective-permute-start = (bf16[2048,512]{1,0:T(8,128)(2,1)}, bf16[2048,512]{1,0:T(8,128)(2,1)}, u32[]{:S(2)}, u32[]{:S(2)}) collective-permute-start(bf16[2048,512]{1,0:T(8,128)(2,1)} %param.8), channel_id=1, source_target_pairs={{0,8},{8,16},{16,24},{24,32},{32,40},{40,48},{48,56},{56,64},{64,7... | collective-permute-start | bytes 6291464 | tf_op jit(solution)/shard_map/ppermute | solution.py:15
  11.9 48.4 %collective-permute-start.1 = (bf16[2048,512]{1,0:T(8,128)(2,1)}, bf16[2048,512]{1,0:T(8,128)(2,1)}, u32[]{:S(2)}, u32[]{:S(2)}) collective-permute-start(bf16[2048,512]{1,0:T(8,128)(2,1)} %param.8), channel_id=1, source_target_pairs={{8,0},{16,8},{24,16},{32,24},{40,32},{48,40},{56,48},{64,56},{72,6... | collective-permute-start | bytes 6291464 | tf_op jit(solution)/shard_map/ppermute | solution.py:18
  81.7 82.0 %copy-start.11 = (f32[512,256]{1,0:T(8,128)S(1)}, f32[512,256]{1,0:T(8,128)}, u32[]{:S(2)}) copy-start(f32[512,256]{1,0:T(8,128)} %param.9) | copy-start | bytes 1572868
  169.3 1.3 copy-start.1
  180.5 4.1 %copy-start.2 = (f32[2048,512]{1,0:T(8,128)S(1)}, f32[2048,512]{1,0:T(8,128)}, u32[]{:S(2)}) copy-start(f32[2048,512]{1,0:T(8,128)} %all-reduce.2.cloned.1.call-done) | copy-start | bytes 12582916
  184.6 4.0 %copy-start.3 = (f32[2048,256]{1,0:T(8,128)}, f32[2048,256]{1,0:T(8,128)S(1)}, u32[]{:S(2)}) copy-start(f32[2048,256]{1,0:T(8,128)S(1)} %convolution_divide_fusion) | copy-start | bytes 6291460
  188.6 1.3 copy-start.7
  188.6 12.7 %collective-permute-start.2 = (f32[256,512]{1,0:T(8,128)S(1)}, f32[256,512]{1,0:T(8,128)}, u32[]{:S(2)}, u32[]{:S(2)}) collective-permute-start(f32[256,512]{1,0:T(8,128)S(1)} %fusion.34), channel_id=1, source_target_pairs={{0,8},{8,0},{16,24},{24,16},{32,40},{40,32},{48,56},{56,48},{64,72... | collective-permute-start | bytes 1572872 | tf_op jit(solution)/shard_map/ppermute | solution.py:24
  204.6 0.8 copy-start.6
  216.3 1.9 copy-start.8
  218.2 15.9 %collective-permute-start.3 = (f32[256,512]{1,0:T(8,128)}, f32[256,512]{1,0:T(8,128)}, u32[]{:S(2)}, u32[]{:S(2)}) collective-permute-start(f32[256,512]{1,0:T(8,128)} %fusion.6), channel_id=1, source_target_pairs={{0,16},{8,24},{16,0},{24,8},{32,48},{40,56},{48,32},{56,40},{64,80... | collective-permute-start | bytes 1572872 | tf_op jit(solution)/shard_map/ppermute | solution.py:24
  237.4 0.8 copy-start.5
  245.8 4.6 %copy-start.9 = (f32[512,256]{1,0:T(8,128)S(1)}, f32[512,256]{1,0:T(8,128)}, u32[]{:S(2)}) copy-start(f32[512,256]{1,0:T(8,128)} %copy-done.8) | copy-start | bytes 1572868
  245.8 5.5 %copy-start.4 = (f32[2048,256]{1,0:T(8,128)S(1)}, f32[2048,256]{1,0:T(8,128)}, u32[]{:S(2)}) copy-start(f32[2048,256]{1,0:T(8,128)} %copy-done.3) | copy-start | bytes 6291460
  250.8 3.5 %copy-start.10 = (f32[256,256]{1,0:T(8,128)}, f32[256,256]{1,0:T(8,128)S(1)}, u32[]{:S(2)}) copy-start(f32[256,256]{1,0:T(8,128)S(1)} %fusion.8) | copy-start | bytes 786436
Sparse Core Ops, SparseCore 0:
  81.8 81.7 all-reduce.1
where the time goes:
time: 266 us; the launch traced here: 261 us
  waiting for transfers between devices  152 us (57%)
  matrix products  60.9 us (23%)
  between operations  17 us (6%)
  local copies, waits for them, and re-layouts  11.5 us (4%)
  starting transfers between devices  10.2 us (4%)
  other arithmetic  9.28 us (3%)
    psum x1, waiting for transfers between devices, on_device(): sample = lax.psum(partial_value, 'samp')  81.9 us
    dot_general x57, matrix products, product(): jnp.dot(left, right, precision=HIGH, preferred_element_type=jnp.float32)  53.8 us
    ppermute x1, waiting for transfers between devices, with_halo(): lax.ppermute(lax.slice_in_dim(block, block.shape[dim] - width, None, axis...  41 us
    ppermute x2, waiting for transfers between devices, swapped(): lax.ppermute(value, axis, [(i, i ^ 1 << distance) for i in range(lax.axis...  24.3 us
    gather x1, local copies, waits for them, and re-layouts, on_device(): picked = jnp.take(blocks, local_columns, axis=0)  8.31 us
    dot_general x1, matrix products, on_device(): jnp.einsum('tkab,tkbs->tas', coupling_tiles, picked, preferred_element_ty...  7.1 us
    concatenate x1, other arithmetic, with_halo(): block = jnp.concatenate([low, block, high], axis=dim)  5.99 us
  transfers between devices with their start and end apart: 5, of which 5 were waited for; matrix products, arithmetic and copies ran while one was open for 0% of the time, Pallas kernels for 0%

commit v1 on v0

--- a/solution.py
+++ b/solution.py
@@ -63,7 +63,9 @@
     samp_count = lax.axis_size("samp")
     samp_index = lax.axis_index("samp")
     share_cols = sample_cols // samp_count
-    sample = lax.psum(partial_value, "samp")
+    sample = partial_value
+    for hop in (1, 2, 4):
+        sample = sample + lax.ppermute(sample, "samp", [(dev, dev ^ hop) for dev in range(8)])
 
     def sketch(stacked, phi_matrix):
         return product(stacked, phi_matrix)

time: 266 us -> 355 us (1.33)
  the two profiles are of different devices: /device:TPU:7 before, /device:TPU:126 now
where the time goes in v1:
time: 355 us; the launch traced here: 349 us
  waiting for transfers between devices  265 us (75%)
  matrix products  51.1 us (14%)
  starting transfers between devices  10.3 us (3%)
  other arithmetic  9.95 us (3%)
  local copies, waits for them, and re-layouts  8.65 us (2%)
  between operations  3.82 us (1%)
    ppermute x3, waiting for transfers between devices, on_device(): lax.ppermute(sample, 'samp', [(dev, dev ^ hop) for dev in range(8)])  191 us
    dot_general x57, matrix products, product(): jnp.dot(left, right, precision=HIGH, preferred_element_type=jnp.float32)  46 us
    ppermute x1, waiting for transfers between devices, with_halo(): lax.ppermute(lax.slice_in_dim(block, block.shape[dim] - width, None, axis...  42.3 us
    ppermute x2, waiting for transfers between devices, swapped(): lax.ppermute(value, axis, [(i, i ^ 1 << distance) for i in range(lax.axis...  24.9 us
    gather x1, local copies, waits for them, and re-layouts, on_device(): picked = jnp.take(blocks, local_columns, axis=0)  8.32 us
    ppermute x1, waiting for transfers between devices, with_halo(): lax.ppermute(lax.slice_in_dim(block, 0, width, axis=dim), axis, backward)  7.44 us
  transfers between devices with their start and end apart: 7, of which 7 were waited for; matrix products, arithmetic and copies ran while one was open for 0% of the time, Pallas kernels for 0%

profile of v1, /device:TPU:126, one launch (start us, length us, event | category | flops | bytes accessed | tf_op | source)
XLA Modules:
  0.0 349.4 jit_solution(10003604525191890933)
XLA Ops:
  0.6 4.8 %collective-permute-start = (bf16[2048,512]{1,0:T(8,128)(2,1)}, bf16[2048,512]{1,0:T(8,128)(2,1)}, u32[]{:S(2)}, u32[]{:S(2)}) collective-permute-start(bf16[2048,512]{1,0:T(8,128)(2,1)} %param.8), channel_id=1, source_target_pairs={{0,8},{8,16},{16,24},{24,32},{32,40},{40,48},{48,56},{56,64},{64,7... | collective-permute-start | bytes 6291464 | tf_op jit(solution)/shard_map/ppermute | solution.py:15
  5.5 1.9 collective-permute-start.1
  7.4 0.7 compare_and_fusion
  8.4 42.3 %collective-permute-done = bf16[2048,512]{1,0:T(8,128)(2,1)} collective-permute-done((bf16[2048,512]{1,0:T(8,128)(2,1)}, bf16[2048,512]{1,0:T(8,128)(2,1)}, u32[]{:S(2)}, u32[]{:S(2)}) %collective-permute-start) | collective-permute-done | bytes 2097184 | tf_op jit(solution)/shard_map/ppermute | solution.py:15
  50.7 7.4 %collective-permute-done.1 = bf16[2048,512]{1,0:T(8,128)(2,1)} collective-permute-done((bf16[2048,512]{1,0:T(8,128)(2,1)}, bf16[2048,512]{1,0:T(8,128)(2,1)}, u32[]{:S(2)}, u32[]{:S(2)}) %collective-permute-start.1) | collective-permute-done | bytes 2097184 | tf_op jit(solution)/shard_map/ppermute | solution.py:18
  58.1 6.0 %pad_maximum_fusion = bf16[6144,512]{1,0:T(8,128)(2,1)} fusion(bf16[2048,512]{1,0:T(8,128)(2,1)} %collective-permute-done.1, bf16[2048,512]{1,0:T(8,128)(2,1)} %param.8, bf16[2048,512]{1,0:T(8,128)(2,1)} %collective-permute-done), kind=kLoop, calls=%fused_computation.4 | loop fusion | flops 18874368 | bytes 12582912 | tf_op jit(solution)/shard_map/concatenate | solution.py:19
  64.1 8.3 %gather_fusion = bf16[64,128,512]{2,1,0:T(8,128)(2,1)} fusion(bf16[48,128,512]{2,1,0:T(8,128)(2,1)} %bitcast.105, s32[1024]{0:T(1024)S(1)} %pad_clamp_fusion), kind=kCustom, calls=%fused_computation | custom fusion | bytes 16777472 | tf_op jit(solution)/shard_map/jit(_take)/gather | solution.py:58
  72.4 5.1 %fusion = f32[16,512,128,1]{1,2,3,0:T(8,128)S(1)} fusion(bf16[16,4,128,128]{3,2,1,0:T(8,128)(2,1)S(1)} %copy-done, bf16[16,4,128,512]{3,2,1,0:T(8,128)(2,1)} %bitcast.106, pred[16,4]{1,0:T(8,128)(4,1)S(1)} %copy.11), kind=kOutput, calls=%fused_computation.1 | convolution fusion | flops 1077936128 | bytes 14680128 | tf_op jit(solution)/shard_map/tkab,tkbs->tas/dot_general | solution.py:59
  77.7 7.1 %collective-permute-done.2 = f32[2048,512]{1,0:T(8,128)S(1)} collective-permute-done((f32[2048,512]{1,0:T(8,128)S(1)}, f32[2048,512]{1,0:T(8,128)S(1)}, u32[]{:S(2)}, u32[]{:S(2)}) %collective-permute-start.2) | collective-permute-done | bytes 4194336 | tf_op jit(solution)/shard_map/ppermute | solution.py:68
  84.8 1.0 bitcast_add_fusion
  85.8 0.9 collective-permute-start.3
  86.7 91.8 %collective-permute-done.3 = f32[2048,512]{1,0:T(8,128)S(1)} collective-permute-done((f32[2048,512]{1,0:T(8,128)S(1)}, f32[2048,512]{1,0:T(8,128)S(1)}, u32[]{:S(2)}, u32[]{:S(2)}) %collective-permute-start.3) | collective-permute-done | bytes 4194336 | tf_op jit(solution)/shard_map/ppermute | solution.py:68
  178.5 1.0 add.47
  179.6 2.0 collective-permute-start.4
  181.5 91.9 %collective-permute-done.4 = f32[2048,512]{1,0:T(8,128)S(1)} collective-permute-done((f32[2048,512]{1,0:T(8,128)S(1)}, f32[2048,512]{1,0:T(8,128)S(1)}, u32[]{:S(2)}, u32[]{:S(2)}) %collective-permute-start.4) | collective-permute-done | bytes 4194336 | tf_op jit(solution)/shard_map/ppermute | solution.py:68
  273.4 1.0 add.48
  274.4 3.5 fusion.26
  277.9 4.1 %multiply_reduce_fusion.2 = (f32[]{:T(128)}, f32[256,256]{1,0:T(8,128)S(1)}) fusion(f32[2048,256]{1,0:T(8,128)S(1)} %fusion.26), kind=kOutput, calls=%fused_computation.50 | convolution fusion | flops 1610743808 | bytes 2359300 | tf_op jit(solution)/shard_map/dot_general | solution.py:28
  283.0 0.4 fusion.16
  283.7 0.4 select_subtract_fusion.13
  286.0 0.4 select_subtract_fusion.11
  286.8 0.6 fusion.31
  287.4 0.4 select_subtract_fusion.10
  288.2 1.9 convolution_divide_fusion
  290.1 3.8 %fusion.34 = f32[256,512]{1,0:T(8,128)S(1)} fusion(f32[2048,256]{1,0:T(8,128)S(1)} %convolution_divide_fusion, f32[2048,512]{1,0:T(8,128)S(1)} %copy-done.3), kind=kOutput, calls=%fused_computation.86 | convolution fusion | flops 3221225472 | bytes 6815744 | tf_op jit(solution)/shard_map/dot_general | solution.py:28
  294.3 12.2 %collective-permute-done.5 = f32[256,512]{1,0:T(8,128)S(1)} collective-permute-done((f32[256,512]{1,0:T(8,128)S(1)}, f32[256,512]{1,0:T(8,128)S(1)}, u32[]{:S(2)}, u32[]{:S(2)}) %collective-permute-start.5) | collective-permute-done | bytes 524320 | tf_op jit(solution)/shard_map/ppermute | solution.py:24
  306.6 1.0 fusion.7
  307.6 1.6 multiply_reduce_fusion.1
  310.3 0.4 fusion.17
  310.9 0.4 select_subtract_fusion.8
  311.3 0.4 fusion.36
  312.1 0.4 select_subtract_fusion.7
  313.3 0.4 select_subtract_fusion.6
  314.5 0.4 select_subtract_fusion.5
  315.2 0.6 convolution_divide_fusion.2
  315.8 1.1 fusion.6
  317.3 12.7 %collective-permute-done.6 = f32[256,512]{1,0:T(8,128)S(1)} collective-permute-done((f32[256,512]{1,0:T(8,128)S(1)}, f32[256,512]{1,0:T(8,128)S(1)}, u32[]{:S(2)}, u32[]{:S(2)}) %collective-permute-start.6) | collective-permute-done | bytes 524320 | tf_op jit(solution)/shard_map/ppermute | solution.py:24
  330.2 2.0 fusion.5
  332.2 1.6 multiply_reduce_fusion
  334.8 0.4 fusion.18
  335.5 0.4 select_subtract_fusion.3
  336.7 0.4 select_subtract_fusion.2
  339.1 0.4 select_subtract_fusion
  339.9 1.8 convolution_divide_fusion.1
  341.7 1.1 fusion.4
  342.7 1.3 fusion.8
  344.1 0.5 fusion.14
  344.6 4.5 %fusion.49 = f32[2048,64]{0,1:T(8,128)} fusion(f32[2048,256]{1,0:T(8,128)} %copy-done.4, f32[256,64]{1,0:T(8,128)S(1)} %fusion.14), kind=kOutput, calls=%fused_computation.101 | convolution fusion | flops 402653184 | bytes 2686976 | tf_op jit(solution)/shard_map/dot_general | solution.py:28
  (56 shorter events, 11.0 us)
Async XLA Ops:
  0.6 71.8 %copy-start = (bf16[16,4,128,128]{3,2,1,0:T(8,128)(2,1)S(1)}, bf16[16,4,128,128]{3,2,1,0:T(8,128)(2,1)}, u32[]{:S(2)}) copy-start(bf16[16,4,128,128]{3,2,1,0:T(8,128)(2,1)} %param.6) | copy-start | bytes 6291460
  0.6 50.0 %collective-permute-start = (bf16[2048,512]{1,0:T(8,128)(2,1)}, bf16[2048,512]{1,0:T(8,128)(2,1)}, u32[]{:S(2)}, u32[]{:S(2)}) collective-permute-start(bf16[2048,512]{1,0:T(8,128)(2,1)} %param.8), channel_id=1, source_target_pairs={{0,8},{8,16},{16,24},{24,32},{32,40},{40,48},{48,56},{56,64},{64,7... | collective-permute-start | bytes 6291464 | tf_op jit(solution)/shard_map/ppermute | solution.py:15
  5.5 52.6 %collective-permute-start.1 = (bf16[2048,512]{1,0:T(8,128)(2,1)}, bf16[2048,512]{1,0:T(8,128)(2,1)}, u32[]{:S(2)}, u32[]{:S(2)}) collective-permute-start(bf16[2048,512]{1,0:T(8,128)(2,1)} %param.8), channel_id=1, source_target_pairs={{8,0},{16,8},{24,16},{32,24},{40,32},{48,40},{56,48},{64,56},{72,6... | collective-permute-start | bytes 6291464 | tf_op jit(solution)/shard_map/ppermute | solution.py:18
  77.5 7.2 %collective-permute-start.2 = (f32[2048,512]{1,0:T(8,128)S(1)}, f32[2048,512]{1,0:T(8,128)S(1)}, u32[]{:S(2)}, u32[]{:S(2)}) collective-permute-start(f32[2048,512]{1,0:T(8,128)S(1)} %bitcast.107), channel_id=1, source_target_pairs={{0,1},{1,0},{2,3},{3,2},{4,5},{5,4},{6,7},{7,6},{8,9},{9,8},{10,11... | collective-permute-start | bytes 12582920 | tf_op jit(solution)/shard_map/ppermute | solution.py:68
  85.8 92.7 %collective-permute-start.3 = (f32[2048,512]{1,0:T(8,128)S(1)}, f32[2048,512]{1,0:T(8,128)S(1)}, u32[]{:S(2)}, u32[]{:S(2)}) collective-permute-start(f32[2048,512]{1,0:T(8,128)S(1)} %bitcast_add_fusion), channel_id=1, source_target_pairs={{0,2},{1,3},{2,0},{3,1},{4,6},{5,7},{6,4},{7,5},{8,10},{9,11},{10,... | collective-permute-start | bytes 12582920 | tf_op jit(solution)/shard_map/ppermute | solution.py:68
  179.5 94.9 %copy-start.9 = (f32[512,256]{1,0:T(8,128)S(1)}, f32[512,256]{1,0:T(8,128)}, u32[]{:S(2)}) copy-start(f32[512,256]{1,0:T(8,128)} %param.9) | copy-start | bytes 1572868
  179.6 93.8 %collective-permute-start.4 = (f32[2048,512]{1,0:T(8,128)S(1)}, f32[2048,512]{1,0:T(8,128)S(1)}, u32[]{:S(2)}, u32[]{:S(2)}) collective-permute-start(f32[2048,512]{1,0:T(8,128)S(1)} %add.47), channel_id=1, source_target_pairs={{0,4},{1,5},{2,6},{3,7},{4,0},{5,1},{6,2},{7,3},{8,12},{9,13},{10,... | collective-permute-start | bytes 12582920 | tf_op jit(solution)/shard_map/ppermute | solution.py:68
  274.4 7.6 %copy-start.2 = (f32[2048,512]{1,0:T(8,128)}, f32[2048,512]{1,0:T(8,128)S(1)}, u32[]{:S(2)}) copy-start(f32[2048,512]{1,0:T(8,128)S(1)} %add.48) | copy-start | bytes 12582916
  287.8 2.3 copy-start.3
  290.1 3.8 %copy-start.4 = (f32[2048,256]{1,0:T(8,128)}, f32[2048,256]{1,0:T(8,128)S(1)}, u32[]{:S(2)}) copy-start(f32[2048,256]{1,0:T(8,128)S(1)} %convolution_divide_fusion) | copy-start | bytes 6291460
  290.1 16.5 %copy-start.8 = (f32[512,256]{1,0:T(8,128)S(1)}, f32[512,256]{1,0:T(8,128)}, u32[]{:S(2)}) copy-start(f32[512,256]{1,0:T(8,128)} %param.10) | copy-start | bytes 1572868
  294.0 12.5 %collective-permute-start.5 = (f32[256,512]{1,0:T(8,128)S(1)}, f32[256,512]{1,0:T(8,128)S(1)}, u32[]{:S(2)}, u32[]{:S(2)}) collective-permute-start(f32[256,512]{1,0:T(8,128)S(1)} %fusion.34), channel_id=1, source_target_pairs={{0,8},{8,0},{16,24},{24,16},{32,40},{40,32},{48,56},{56,48},{64,72... | collective-permute-start | bytes 1572872 | tf_op jit(solution)/shard_map/ppermute | solution.py:24
  315.8 19.0 %copy-start.6 = (f32[512,256]{1,0:T(8,128)}, f32[512,256]{1,0:T(8,128)S(1)}, u32[]{:S(2)}) copy-start(f32[512,256]{1,0:T(8,128)S(1)} %convolution_divide_fusion.2) | copy-start | bytes 1572868
  316.9 13.1 %collective-permute-start.6 = (f32[256,512]{1,0:T(8,128)S(1)}, f32[256,512]{1,0:T(8,128)S(1)}, u32[]{:S(2)}, u32[]{:S(2)}) collective-permute-start(f32[256,512]{1,0:T(8,128)S(1)} %fusion.6), channel_id=1, source_target_pairs={{0,16},{8,24},{16,0},{24,8},{32,48},{40,56},{48,32},{56,40},{64,80... | collective-permute-start | bytes 1572872 | tf_op jit(solution)/shard_map/ppermute | solution.py:24
  332.2 5.7 %copy-start.5 = (f32[512,256]{1,0:T(8,128)}, f32[512,256]{1,0:T(8,128)S(1)}, u32[]{:S(2)}) copy-start(f32[512,256]{1,0:T(8,128)S(1)} %fusion.5) | copy-start | bytes 1572868
  339.5 9.7 %copy-start.1 = (bf16[16,4,128,128]{3,2,1,0:T(8,128)(2,1)S(1)}, bf16[16,4,128,128]{3,2,1,0:T(8,128)(2,1)}, u32[]{:S(2)}) copy-start(bf16[16,4,128,128]{3,2,1,0:T(8,128)(2,1)} %param.6) | copy-start | bytes 6291460
  344.1 5.0 %copy-start.7 = (f32[256,256]{1,0:T(8,128)}, f32[256,256]{1,0:T(8,128)S(1)}, u32[]{:S(2)}) copy-start(f32[256,256]{1,0:T(8,128)S(1)} %fusion.8) | copy-start | bytes 786436
